TPU v7x, 32 devices: a whole 2x2x4 slice. The times are simulated.
32 devices in a mesh: row: 4 (over z), col: 8 (over y, x, core).
Axes of the slice: x: 2, y: 2, z: 4, core: 2. Of those that a mesh axis runs over, the one named last changes fastest.
Arguments:
- right_side: float32 [64, 16384], P(None, ('row', 'col')), may hold values from -80 to 80
- diag_vals: float32 [16384], P(('row', 'col')), may hold values from 1.05 to 1.6
- tiles: bfloat16 [64, 16, 256, 256], P(('row', 'col')), may hold values from -1 to 1, as said below
- col_ids: int32 [64, 16], P(('row', 'col')), may hold values from 0 to 63, as said below
Outputs:
- solution: float32 [64, 16384], P(None, ('row', 'col'))
- residual: float32 [64, 16384], P(None, ('row', 'col'))
Inputs may be any that keep to these rules, and one draw needn't show every extreme that they name: col_ids[i, m] = (i + o_m) mod 64 and col_ids[i, 8 + m] = (i - o_m) mod 64 for 8 distinct odd offsets o_m shared by all block-rows, each below 32. The pattern is symmetric. tiles[i, m] is the block in block-row i and block-column col_ids[i, m]; tiles[i, 8 + m] is the transpose of tiles[(i - o_m) mod 64, m], so the matrix is symmetric.
All inputs are finite; a program needn't handle non-finite values.
Results may differ from a plain program's by a relative error of at most 0.00062.
Values may be sent and summed in bfloat16 or wider, within the bound.
No kernel may reach another device: no remote copies, remote signals or barrier semaphores. Data moves between devices by JAX's collectives and lax.ppermute only.
A program may use at most 64 MiB of HBM per device.

v0:
```python
import jax
import jax.numpy as jnp
from jax import lax
from jax.sharding import PartitionSpec as P

ITERS = 4


def chol_solve(mat, rhs):
    lower = jnp.linalg.cholesky(mat)
    half = lax.linalg.triangular_solve(lower, rhs, left_side=True, lower=True)
    return lax.linalg.triangular_solve(lower, half, left_side=True, lower=True, transpose_a=True)


def gram_of(left, right):
    return jnp.dot(
        left, right.T, precision=lax.Precision.HIGHEST, preferred_element_type=jnp.float32
    )


def small_dot(left, right):
    return jnp.dot(left, right, precision=lax.Precision.HIGHEST, preferred_element_type=jnp.float32)


def apply_matrix(vec, diag_vals, tiles, col_ids):
    rhs_count = vec.shape[0]
    rows_here = tiles.shape[0]
    nbr = tiles.shape[1]
    blk = tiles.shape[2]
    rounded = vec.astype(jnp.bfloat16).reshape(rhs_count, rows_here, blk)
    whole = lax.all_gather(
        rounded.reshape(rhs_count, rows_here * blk), ("row", "col"), axis=1, tiled=True
    )
    whole = whole.reshape(rhs_count, -1, blk)
    picked = jnp.take(whole, col_ids.reshape(-1), axis=1).reshape(rhs_count, rows_here, nbr, blk)
    off = jnp.einsum("srkb,rkab->sra", picked, tiles, preferred_element_type=jnp.float32)
    coef = 1.0 / (nbr * blk)
    return diag_vals[None, :] * vec + coef * off.reshape(rhs_count, rows_here * blk)


def body(right_side, diag_vals, tiles, col_ids):
    solution = jnp.zeros_like(right_side)
    residual = right_side
    direction = right_side
    gram = lax.psum(gram_of(residual, residual), ("row", "col"))
    for step in range(ITERS):
        image = apply_matrix(direction, diag_vals, tiles, col_ids)
        curv = lax.psum(gram_of(direction, image), ("row", "col"))
        alpha = chol_solve(curv, gram)
        solution = solution + small_dot(alpha.T, direction)
        residual = residual - small_dot(alpha.T, image)
        if step + 1 < ITERS:
            gram_new = lax.psum(gram_of(residual, residual), ("row", "col"))
            beta = chol_solve(gram, gram_new)
            direction = residual + small_dot(beta.T, direction)
            gram = gram_new
    return (solution, residual)


def solution(mesh):
    placed = (
        P(None, ("row", "col")),
        P(("row", "col")),
        P(("row", "col"), None, None, None),
        P(("row", "col"), None),
    )
    return jax.shard_map(
        body,
        mesh=mesh,
        in_specs=placed,
        out_specs=(P(None, ("row", "col")), P(None, ("row", "col"))),
        check_vma=False,
    )
```

profile of v0, /device:TPU:0, one launch (start us, length us, event | category | flops | bytes accessed | tf_op | source)
XLA Modules:
  0.0 618.0 jit_solution(6379712227797717869)
XLA Ops:
  7.2 1.5 convert_element_type.12
  8.8 0.8 reshape.70
  9.6 1.2 fusion.64
  10.9 58.3 %all-gather.5.cloned.1.call-done = bf16[64,16384]{1,0:T(8,128)(2,1)} async-done(((bf16[64,512]{1,0:T(8,128)(2,1)}), bf16[64,16384]{1,0:T(8,128)(2,1)}) %all-gather.5.cloned.1.call-update) | async-done | bytes 2097168 | tf_op jit(solution)/shard_map/all_gather | solution.py:31
  69.2 1.9 copy.89
  71.9 3.6 fusion.7
  75.8 40.2 %all-reduce = (f32[64,64]{0,1:T(8,128)S(1)}, f32[64,64]{0,1:T(8,128)S(1)}) all-reduce(f32[64,64]{0,1:T(8,128)S(1)} %fusion.64, f32[64,64]{0,1:T(8,128)S(1)} %convolution_bitcast_fusion.4), channel_id=1, replica_groups=mesh['row'=4,'col'=8] {'row','col'}, use_global_device_ids=true, to_apply=%region_3.6 | all-reduce | flops 8192 | bytes 65536 | tf_op jit(solution)/shard_map/psum | solution.py:45
  116.1 5.8 cholesky.119
  122.0 0.6 compare_reduce_fusion.6
  122.7 0.7 fusion.19
  123.3 4.9 custom-call.21
  129.3 39.6 %psum.58 = f32[64,64]{0,1:T(8,128)S(1)} all-reduce(f32[64,64]{0,1:T(8,128)S(1)} %fusion.66), channel_id=1, replica_groups=mesh['row'=4,'col'=8] {'row','col'}, use_global_device_ids=true, to_apply=%region_4.9 | all-reduce | flops 4096 | bytes 32768 | tf_op jit(solution)/shard_map/psum | solution.py:53
  168.9 5.8 cholesky.130
  175.4 0.7 fusion.20
  176.1 4.9 custom-call.23
  181.4 1.0 fusion.61
  182.5 5.8 cholesky.152
  188.4 0.7 compare_reduce_fusion.3
  189.7 5.5 custom-call.27
  195.2 42.8 %all-gather.7.cloned.1.call-done = bf16[64,16384]{1,0:T(8,128)(2,1)} async-done(((bf16[64,512]{1,0:T(8,128)(2,1)}), bf16[64,16384]{1,0:T(8,128)(2,1)}) %all-gather.7.cloned.1.call-update) | async-done | bytes 2097168 | tf_op jit(solution)/shard_map/all_gather | solution.py:31
  238.0 1.9 copy.88
  240.7 3.6 fusion.6
  244.6 40.0 %psum.59 = f32[64,64]{0,1:T(8,128)S(1)} all-reduce(f32[64,64]{0,1:T(8,128)S(1)} %fusion.8), channel_id=1, replica_groups=mesh['row'=4,'col'=8] {'row','col'}, use_global_device_ids=true, to_apply=%region_5.10 | all-reduce | flops 4096 | bytes 32768 | tf_op jit(solution)/shard_map/psum | solution.py:48
  284.7 5.8 cholesky.141
  291.2 0.7 fusion.21
  291.9 4.9 custom-call.25
  297.8 39.6 %psum.60 = f32[64,64]{0,1:T(8,128)S(1)} all-reduce(f32[64,64]{0,1:T(8,128)S(1)} %fusion.67), channel_id=1, replica_groups=mesh['row'=4,'col'=8] {'row','col'}, use_global_device_ids=true, to_apply=%region_6.11 | all-reduce | flops 4096 | bytes 32768 | tf_op jit(solution)/shard_map/psum | solution.py:53
  337.9 1.0 fusion.62
  339.0 5.8 cholesky.174
  346.1 5.5 custom-call.31
  351.6 42.8 %all-gather.9.cloned.1.call-done = bf16[64,16384]{1,0:T(8,128)(2,1)} async-done(((bf16[64,512]{1,0:T(8,128)(2,1)}), bf16[64,16384]{1,0:T(8,128)(2,1)}) %all-gather.9.cloned.1.call-update) | async-done | bytes 2097168 | tf_op jit(solution)/shard_map/all_gather | solution.py:31
  394.5 1.9 copy.87
  397.2 3.6 fusion.5
  401.1 39.8 %psum.61 = f32[64,64]{0,1:T(8,128)S(1)} all-reduce(f32[64,64]{0,1:T(8,128)S(1)} %fusion.9), channel_id=1, replica_groups=mesh['row'=4,'col'=8] {'row','col'}, use_global_device_ids=true, to_apply=%region_7.12 | all-reduce | flops 4096 | bytes 32768 | tf_op jit(solution)/shard_map/psum | solution.py:48
  441.0 5.8 cholesky.163
  447.5 0.7 fusion.23
  448.2 4.9 custom-call.29
  454.1 39.9 %psum.62 = f32[64,64]{1,0:T(8,128)S(1)} all-reduce(f32[64,64]{1,0:T(8,128)S(1)} %fusion.68), channel_id=1, replica_groups=mesh['row'=4,'col'=8] {'row','col'}, use_global_device_ids=true, to_apply=%region_8.13 | all-reduce | flops 4096 | bytes 32768 | tf_op jit(solution)/shard_map/psum | solution.py:53
  494.4 0.9 fusion.63
  496.4 54.1 %all-gather.11.cloned.1.call-done = bf16[64,16384]{1,0:T(8,128)(2,1)} async-done(((bf16[64,512]{1,0:T(8,128)(2,1)}), bf16[64,16384]{1,0:T(8,128)(2,1)}) %all-gather.11.cloned.1.call-update) | async-done | bytes 2097168 | tf_op jit(solution)/shard_map/all_gather | solution.py:31
  550.5 1.9 copy.86
  553.2 3.6 fusion.4
  557.1 39.8 %psum.63 = f32[64,64]{0,1:T(8,128)S(1)} all-reduce(f32[64,64]{0,1:T(8,128)S(1)} %fusion.10), channel_id=1, replica_groups=mesh['row'=4,'col'=8] {'row','col'}, use_global_device_ids=true, to_apply=%region_9.14 | all-reduce | flops 4096 | bytes 32768 | tf_op jit(solution)/shard_map/psum | solution.py:48
  597.0 5.8 cholesky.185
  603.5 0.7 fusion.25
  604.2 4.9 custom-call.33
  609.5 1.0 convolution_subtract_fusion
  610.5 1.0 convolution_add_fusion
  (109 shorter events, 15.3 us)
Async XLA Ops:
  7.2 62.0 %all-gather.5.cloned.1.call-start = ((), (), s32[]{:S(2)}) async-start(), calls=%async_computation | async-start | bytes 2162688 | tf_op jit(solution)/shard_map/all_gather | solution.py:31
  8.8 229.2 %all-gather.7.cloned.1.call-start = ((), (), s32[]{:S(2)}) async-start(), calls=%async_computation.1 | async-start | bytes 2162688 | tf_op jit(solution)/shard_map/all_gather | solution.py:31
  71.7 3.8 copy-start
  71.7 3.8 copy-start.13
  128.6 109.4 %copy-start.9 = (f32[64,64]{1,0:T(8,128)}, f32[64,64]{1,0:T(8,128)S(1)}, u32[]{:S(2)}) copy-start(f32[64,64]{1,0:T(8,128)S(1)} %fusion.58) | copy-start | bytes 49156
  168.9 71.0 %copy-start.3 = (f32[64,64]{0,1:T(8,128)}, f32[64,64]{0,1:T(8,128)S(1)}, u32[]{:S(2)}) copy-start(f32[64,64]{0,1:T(8,128)S(1)} %psum.58) | copy-start | bytes 49156
  182.4 212.1 %all-gather.9.cloned.1.call-start = ((), (), s32[]{:S(2)}) async-start(), calls=%async_computation.2 | async-start | bytes 2162688 | tf_op jit(solution)/shard_map/all_gather | solution.py:31
  240.5 56.3 %copy-start.4 = (f32[64,64]{0,1:T(8,128)S(1)}, f32[64,64]{0,1:T(8,128)}, u32[]{:S(2)}) copy-start(f32[64,64]{0,1:T(8,128)} %copy-done.3) | copy-start | bytes 49156
  240.7 96.8 %copy-start.14 = (f32[1,64,64]{1,2,0:T(8,128)S(1)}, f32[1,64,64]{1,2,0:T(8,128)}, u32[]{:S(2)}) copy-start(f32[1,64,64]{1,2,0:T(8,128)} %custom-call.27) | copy-start | bytes 49156
  297.2 99.1 %copy-start.11 = (f32[64,64]{1,0:T(8,128)}, f32[64,64]{1,0:T(8,128)S(1)}, u32[]{:S(2)}) copy-start(f32[64,64]{1,0:T(8,128)S(1)} %fusion.48) | copy-start | bytes 49156
  297.5 98.8 %copy-start.1 = (f32[64,512]{1,0:T(8,128)}, f32[64,512]{1,0:T(8,128)S(1)}, u32[]{:S(2)}) copy-start(f32[64,512]{1,0:T(8,128)S(1)} %convolution_subtract_fusion.2) | copy-start | bytes 393220
  337.5 57.0 %copy-start.5 = (f32[64,64]{0,1:T(8,128)}, f32[64,64]{0,1:T(8,128)S(1)}, u32[]{:S(2)}) copy-start(f32[64,64]{0,1:T(8,128)S(1)} %psum.60) | copy-start | bytes 49156
  338.9 211.6 %all-gather.11.cloned.1.call-start = ((), (), s32[]{:S(2)}) async-start(), calls=%async_computation.3 | async-start | bytes 2162688 | tf_op jit(solution)/shard_map/all_gather | solution.py:31
  397.0 56.1 %copy-start.6 = (f32[64,64]{0,1:T(8,128)S(1)}, f32[64,64]{0,1:T(8,128)}, u32[]{:S(2)}) copy-start(f32[64,64]{0,1:T(8,128)} %copy-done.5) | copy-start | bytes 49156
  397.0 56.5 %copy-start.2 = (f32[64,512]{1,0:T(8,128)S(1)}, f32[64,512]{1,0:T(8,128)}, u32[]{:S(2)}) copy-start(f32[64,512]{1,0:T(8,128)} %copy-done.1) | copy-start | bytes 393220
  397.2 96.8 %copy-start.15 = (f32[1,64,64]{1,2,0:T(8,128)S(1)}, f32[1,64,64]{1,2,0:T(8,128)}, u32[]{:S(2)}) copy-start(f32[1,64,64]{1,2,0:T(8,128)} %custom-call.31) | copy-start | bytes 49156
  397.2 98.2 %copy-start.10 = (f32[64,64]{1,0:T(8,128)S(1)}, f32[64,64]{1,0:T(8,128)}, u32[]{:S(2)}) copy-start(f32[64,64]{1,0:T(8,128)} %copy-done.9) | copy-start | bytes 49156
  397.2 98.6 %copy-start.12 = (f32[64,64]{1,0:T(8,128)S(1)}, f32[64,64]{1,0:T(8,128)}, u32[]{:S(2)}) copy-start(f32[64,64]{1,0:T(8,128)} %copy-done.11) | copy-start | bytes 49156
  494.0 1.4 copy-start.7
  553.0 56.1 %copy-start.8 = (f32[64,64]{1,0:T(8,128)S(1)}, f32[64,64]{1,0:T(8,128)}, u32[]{:S(2)}) copy-start(f32[64,64]{1,0:T(8,128)} %copy-done.7) | copy-start | bytes 49156
Sparse Core Ops, SparseCore 0:
  11.5 57.6 all-gather.4
  182.5 55.4 all-gather.6
  339.0 55.4 all-gather.8
  495.5 54.9 all-gather.10
where the time goes:
time: 619 us; the launch traced here: 618 us
  blocking collectives  279 us (45%)
  waiting for transfers between devices  198 us (32%)
  other arithmetic  87.9 us (14%)
  matrix products  26.9 us (4%)
  between operations  14.6 us (2%)
  local copies, waits for them, and re-layouts  11.3 us (2%)
    all_gather x4, waiting for transfers between devices, apply_matrix(): lax.all_gather(rounded.reshape(rhs_count, rows_here * blk), ('row', 'col'...  198 us
    psum x3, blocking collectives, body(): curv = lax.psum(gram_of(direction, image), ('row', 'col'))  120 us
    psum x3, blocking collectives, body(): gram_new = lax.psum(gram_of(residual, residual), ('row', 'col'))  119 us
    another operation x21, other arithmetic, chol_solve(): lower = jnp.linalg.cholesky(mat)  45.6 us
    psum x1, blocking collectives, body(): gram = lax.psum(gram_of(residual, residual), ('row', 'col'))  40.2 us
    another operation x14, other arithmetic, chol_solve(): lax.linalg.triangular_solve(lower, half, left_side=True, lower=True, tran...  40 us
    dot_general x4, matrix products, apply_matrix(): jnp.einsum('srkb,rkab->sra', picked, tiles, preferred_element_type=jnp.fl...  14.3 us
  transfers between devices with their start and end apart: 4, of which 4 were waited for; matrix products, arithmetic and copies ran while one was open for 5% of the time, Pallas kernels for 0%

commit v1 on v0

--- a/solution.py
+++ b/solution.py
@@ -45,7 +45,7 @@
     gram = lax.psum(gram_of(residual, residual), ("row", "col"))
     for step in range(ITERS):
         image = apply_matrix(direction, diag_vals, tiles, col_ids)
-        curv = lax.psum(gram_of(direction, image), ("row", "col"))
+        curv = jnp.sum(lax.all_gather(gram_of(direction, image), ("row", "col")), axis=0)
         alpha = chol_solve(curv, gram)
         solution = solution + small_dot(alpha.T, direction)
         residual = residual - small_dot(alpha.T, image)

time: 619 us -> 611 us (0.987)
  waiting for transfers between devices: 198 us -> 145 us
  blocking collectives: 279 us -> 324 us
    all_gather x0 -> x4, blocking collectives: none -> 170 us  [body(): lax.all_gather(gram_of(direction, image), ('row', 'col'))]
    psum x3 -> x0, blocking collectives: 120 us -> none  [body(): curv = lax.psum(gram_of(direction, image), ('row', 'col'))]
    all_gather x4, waiting for transfers between devices: 198 us -> 145 us  [apply_matrix(): lax.all_gather(rounded.reshape(rhs_count, rows_here * blk), ('row', 'col'...]
    psum x3, blocking collectives: 119 us -> 111 us  [body(): gram_new = lax.psum(gram_of(residual, residual), ('row', 'col'))]
  transfers between devices with their start and end apart: 4 -> 4, of which waited for: 4 -> 4; matrix products, arithmetic and copies ran while one was open for 5% -> 7% of each run, Pallas kernels for 0% -> 0%
where the time goes in v1:
time: 611 us; the launch traced here: 610 us
  blocking collectives  324 us (53%)
  waiting for transfers between devices  145 us (24%)
  other arithmetic  88.2 us (14%)
  matrix products  26.9 us (4%)
  between operations  14.5 us (2%)
  local copies, waits for them, and re-layouts  11.7 us (2%)
    all_gather x4, blocking collectives, body(): lax.all_gather(gram_of(direction, image), ('row', 'col'))  170 us
    all_gather x4, waiting for transfers between devices, apply_matrix(): lax.all_gather(rounded.reshape(rhs_count, rows_here * blk), ('row', 'col'...  145 us
    psum x3, blocking collectives, body(): gram_new = lax.psum(gram_of(residual, residual), ('row', 'col'))  111 us
    another operation x21, other arithmetic, chol_solve(): lower = jnp.linalg.cholesky(mat)  45.6 us
    psum x1, blocking collectives, body(): gram = lax.psum(gram_of(residual, residual), ('row', 'col'))  42.2 us
    another operation x14, other arithmetic, chol_solve(): lax.linalg.triangular_solve(lower, half, left_side=True, lower=True, tran...  40 us
    dot_general x4, matrix products, apply_matrix(): jnp.einsum('srkb,rkab->sra', picked, tiles, preferred_element_type=jnp.fl...  14.3 us
  transfers between devices with their start and end apart: 4, of which 4 were waited for; matrix products, arithmetic and copies ran while one was open for 7% of the time, Pallas kernels for 0%

profile of v1, /device:TPU:0, one launch (start us, length us, event | category | flops | bytes accessed | tf_op | source)
XLA Modules:
  0.0 610.3 jit_solution(7515138962895974362)
XLA Ops:
  7.2 1.5 convert_element_type.12
  8.8 0.8 reshape.70
  9.6 1.2 fusion.64
  10.8 42.2 %psum.28 = f32[64,64]{0,1:T(8,128)S(1)} all-reduce(f32[64,64]{0,1:T(8,128)S(1)} %fusion.64), channel_id=1, replica_groups=mesh['row'=4,'col'=8] {'row','col'}, use_global_device_ids=true, to_apply=%region_3.6 | all-reduce | flops 4096 | bytes 32768 | tf_op jit(solution)/shard_map/psum | solution.py:45
  53.1 5.8 cholesky.130
  59.6 0.7 fusion.20
  60.3 4.9 custom-call.23
  65.2 4.1 all-gather.9.cloned.1.call-done
  69.3 1.9 copy.115
  72.0 3.6 fusion.7
  75.9 42.6 %all-gather = f32[2048,64]{1,0:T(8,128)S(1)} all-gather(f32[64,64]{1,0:T(8,128)S(1)} %copy.76), channel_id=2, replica_groups=mesh['row'=4,'col'=8] {'row','col'}, dimensions={0}, use_global_device_ids=true | all-gather | bytes 540672 | tf_op jit(solution)/shard_map/all_gather | solution.py:48
  118.7 5.8 cholesky.119
  125.3 0.7 fusion.19
  125.9 4.9 custom-call.21
  131.9 37.0 %psum.29 = f32[64,64]{0,1:T(8,128)S(1)} all-reduce(f32[64,64]{0,1:T(8,128)S(1)} %fusion.66), channel_id=1, replica_groups=mesh['row'=4,'col'=8] {'row','col'}, use_global_device_ids=true, to_apply=%region_4.9 | all-reduce | flops 4096 | bytes 32768 | tf_op jit(solution)/shard_map/psum | solution.py:53
  169.3 1.0 fusion.61
  170.5 5.8 cholesky.152
  176.3 0.7 compare_reduce_fusion.3
  177.6 5.5 custom-call.27
  183.1 43.1 %all-gather.11.cloned.1.call-done = bf16[64,16384]{1,0:T(8,128)(2,1)} async-done(((bf16[64,512]{1,0:T(8,128)(2,1)}), bf16[64,16384]{1,0:T(8,128)(2,1)}) %all-gather.11.cloned.1.call-update) | async-done | bytes 2097168 | tf_op jit(solution)/shard_map/all_gather | solution.py:31
  226.2 1.9 copy.114
  228.9 3.6 fusion.6
  232.7 42.7 %all-gather.1 = f32[2048,64]{1,0:T(8,128)S(1)} all-gather(f32[64,64]{1,0:T(8,128)S(1)} %fusion.8), channel_id=3, replica_groups=mesh['row'=4,'col'=8] {'row','col'}, dimensions={0}, use_global_device_ids=true | all-gather | bytes 540672 | tf_op jit(solution)/shard_map/all_gather | solution.py:48
  275.6 5.8 cholesky.141
  282.2 0.7 fusion.21
  282.8 4.9 custom-call.25
  289.0 37.0 %psum.30 = f32[64,64]{0,1:T(8,128)S(1)} all-reduce(f32[64,64]{0,1:T(8,128)S(1)} %fusion.67), channel_id=1, replica_groups=mesh['row'=4,'col'=8] {'row','col'}, use_global_device_ids=true, to_apply=%region_6.11 | all-reduce | flops 4096 | bytes 32768 | tf_op jit(solution)/shard_map/psum | solution.py:53
  326.5 1.0 fusion.62
  327.6 5.8 cholesky.174
  334.7 5.5 custom-call.31
  340.2 43.0 %all-gather.13.cloned.1.call-done = bf16[64,16384]{1,0:T(8,128)(2,1)} async-done(((bf16[64,512]{1,0:T(8,128)(2,1)}), bf16[64,16384]{1,0:T(8,128)(2,1)}) %all-gather.13.cloned.1.call-update) | async-done | bytes 2097168 | tf_op jit(solution)/shard_map/all_gather | solution.py:31
  383.3 1.9 copy.113
  386.0 3.6 fusion.5
  389.9 42.5 %all-gather.2 = f32[2048,64]{1,0:T(8,128)S(1)} all-gather(f32[64,64]{1,0:T(8,128)S(1)} %fusion.9), channel_id=4, replica_groups=mesh['row'=4,'col'=8] {'row','col'}, dimensions={0}, use_global_device_ids=true | all-gather | bytes 540672 | tf_op jit(solution)/shard_map/all_gather | solution.py:48
  432.7 5.8 cholesky.163
  439.2 0.7 fusion.23
  439.9 4.9 custom-call.29
  445.8 37.3 %psum.31 = f32[64,64]{1,0:T(8,128)S(1)} all-reduce(f32[64,64]{1,0:T(8,128)S(1)} %fusion.68), channel_id=1, replica_groups=mesh['row'=4,'col'=8] {'row','col'}, use_global_device_ids=true, to_apply=%region_8.13 | all-reduce | flops 4096 | bytes 32768 | tf_op jit(solution)/shard_map/psum | solution.py:53
  483.5 0.9 fusion.63
  485.5 54.6 %all-gather.15.cloned.1.call-done = bf16[64,16384]{1,0:T(8,128)(2,1)} async-done(((bf16[64,512]{1,0:T(8,128)(2,1)}), bf16[64,16384]{1,0:T(8,128)(2,1)}) %all-gather.15.cloned.1.call-update) | async-done | bytes 2097168 | tf_op jit(solution)/shard_map/all_gather | solution.py:31
  540.1 1.9 copy.112
  542.7 3.6 fusion.4
  546.6 42.5 %all-gather.3 = f32[2048,64]{1,0:T(8,128)S(1)} all-gather(f32[64,64]{1,0:T(8,128)S(1)} %fusion.10), channel_id=5, replica_groups=mesh['row'=4,'col'=8] {'row','col'}, dimensions={0}, use_global_device_ids=true | all-gather | bytes 540672 | tf_op jit(solution)/shard_map/all_gather | solution.py:48
  589.3 5.8 cholesky.185
  595.9 0.7 fusion.25
  596.5 4.9 custom-call.33
  601.8 1.0 convolution_subtract_fusion
  602.8 1.0 convolution_add_fusion
  (116 shorter events, 16.6 us)
Async XLA Ops:
  7.2 62.1 %all-gather.9.cloned.1.call-start = ((), (), s32[]{:S(2)}) async-start(), calls=%async_computation | async-start | bytes 2162688 | tf_op jit(solution)/shard_map/all_gather | solution.py:31
  8.8 217.4 %all-gather.11.cloned.1.call-start = ((), (), s32[]{:S(2)}) async-start(), calls=%async_computation.1 | async-start | bytes 2162688 | tf_op jit(solution)/shard_map/all_gather | solution.py:31
  71.8 3.8 copy-start
  71.8 3.8 copy-start.13
  131.3 94.9 %copy-start.9 = (f32[64,64]{1,0:T(8,128)}, f32[64,64]{1,0:T(8,128)S(1)}, u32[]{:S(2)}) copy-start(f32[64,64]{1,0:T(8,128)S(1)} %fusion.58) | copy-start | bytes 49156
  168.9 59.1 %copy-start.3 = (f32[64,64]{0,1:T(8,128)}, f32[64,64]{0,1:T(8,128)S(1)}, u32[]{:S(2)}) copy-start(f32[64,64]{0,1:T(8,128)S(1)} %psum.29) | copy-start | bytes 49156
  170.3 213.0 %all-gather.13.cloned.1.call-start = ((), (), s32[]{:S(2)}) async-start(), calls=%async_computation.2 | async-start | bytes 2162688 | tf_op jit(solution)/shard_map/all_gather | solution.py:31
  228.9 58.9 %copy-start.4 = (f32[64,64]{0,1:T(8,128)S(1)}, f32[64,64]{0,1:T(8,128)}, u32[]{:S(2)}) copy-start(f32[64,64]{0,1:T(8,128)} %copy-done.3) | copy-start | bytes 49156
  228.9 97.2 %copy-start.14 = (f32[1,64,64]{1,2,0:T(8,128)S(1)}, f32[1,64,64]{1,2,0:T(8,128)}, u32[]{:S(2)}) copy-start(f32[1,64,64]{1,2,0:T(8,128)} %custom-call.27) | copy-start | bytes 49156
  288.2 0.6 copy-start.11
  288.8 94.5 %copy-start.1 = (f32[64,512]{1,0:T(8,128)}, f32[64,512]{1,0:T(8,128)S(1)}, u32[]{:S(2)}) copy-start(f32[64,512]{1,0:T(8,128)S(1)} %convolution_subtract_fusion.2) | copy-start | bytes 393220
  326.1 57.2 %copy-start.5 = (f32[64,64]{0,1:T(8,128)}, f32[64,64]{0,1:T(8,128)S(1)}, u32[]{:S(2)}) copy-start(f32[64,64]{0,1:T(8,128)S(1)} %psum.30) | copy-start | bytes 49156
  327.5 212.6 %all-gather.15.cloned.1.call-start = ((), (), s32[]{:S(2)}) async-start(), calls=%async_computation.3 | async-start | bytes 2162688 | tf_op jit(solution)/shard_map/all_gather | solution.py:31
  386.0 58.8 %copy-start.6 = (f32[64,64]{0,1:T(8,128)S(1)}, f32[64,64]{0,1:T(8,128)}, u32[]{:S(2)}) copy-start(f32[64,64]{0,1:T(8,128)} %copy-done.5) | copy-start | bytes 49156
  386.0 59.2 %copy-start.2 = (f32[64,512]{1,0:T(8,128)S(1)}, f32[64,512]{1,0:T(8,128)}, u32[]{:S(2)}) copy-start(f32[64,512]{1,0:T(8,128)} %copy-done.1) | copy-start | bytes 393220
  386.0 97.1 %copy-start.15 = (f32[1,64,64]{1,2,0:T(8,128)S(1)}, f32[1,64,64]{1,2,0:T(8,128)}, u32[]{:S(2)}) copy-start(f32[1,64,64]{1,2,0:T(8,128)} %custom-call.31) | copy-start | bytes 49156
  386.0 98.5 %copy-start.10 = (f32[64,64]{1,0:T(8,128)S(1)}, f32[64,64]{1,0:T(8,128)}, u32[]{:S(2)}) copy-start(f32[64,64]{1,0:T(8,128)} %copy-done.9) | copy-start | bytes 49156
  386.0 98.8 %copy-start.12 = (f32[64,64]{1,0:T(8,128)S(1)}, f32[64,64]{1,0:T(8,128)}, u32[]{:S(2)}) copy-start(f32[64,64]{1,0:T(8,128)} %copy-done.11) | copy-start | bytes 49156
  483.1 1.4 copy-start.7
  542.7 58.7 %copy-start.8 = (f32[64,64]{1,0:T(8,128)S(1)}, f32[64,64]{1,0:T(8,128)}, u32[]{:S(2)}) copy-start(f32[64,64]{1,0:T(8,128)} %copy-done.7) | copy-start | bytes 49156
Sparse Core Ops, SparseCore 0:
  11.5 57.7 all-gather.8
  170.4 55.7 all-gather.10
  327.6 55.6 all-gather.12
  484.6 55.4 all-gather.14
